TPU v7x, 32 devices: a whole 2x2x4 slice. The times are simulated.
32 devices in a mesh: dp: 16 (over z, y, x), mp: 2 (over core).
Axes of the slice: x: 2, y: 2, z: 4, core: 2. Of those that a mesh axis runs over, the one named last changes fastest.
Arguments:
- tokens: bfloat16 [16384, 768], P(('dp', 'mp')), may hold values from -8 to 8
- segment_ids: int32 [16, 1024], P('dp'), may hold values from 0 to 16, never falling along the last dimension, each value on 1 to 512 neighbouring positions
- query_weight: bfloat16 [768, 768], P(None, 'mp'), may hold values from -0.21875 to 0.21875
- key_weight: bfloat16 [768, 768], P(None, 'mp'), may hold values from -0.21875 to 0.21875
- value_weight: bfloat16 [768, 768], P(None, 'mp'), may hold values from -0.21875 to 0.21875
- output_weight: bfloat16 [768, 768], P('mp'), may hold values from -0.875 to 0.875
- inner_weight: bfloat16 [768, 3072], P(None, 'mp'), may hold values from -0.21875 to 0.21875
- outer_weight: bfloat16 [3072, 768], P('mp'), may hold values from -0.109375 to 0.109375
- mixer_down: bfloat16 [768, 64], replicated, may hold values from -0.21875 to 0.21875
- mixer_down_bias: bfloat16 [64], replicated, may hold values from -3 to 3
- mixer_up: bfloat16 [64, 768], replicated, may hold values from -0.75 to 0.75
- mixer_up_bias: bfloat16 [768], replicated, may hold values from -3 to 3
- dense_down: bfloat16 [768, 64], replicated, may hold values from -0.21875 to 0.21875
- dense_down_bias: bfloat16 [64], replicated, may hold values from -3 to 3
- dense_up: bfloat16 [64, 768], replicated, may hold values from -0.75 to 0.75
- dense_up_bias: bfloat16 [768], replicated, may hold values from -3 to 3
- first_gain: bfloat16 [768], replicated, may hold values from 0.5 to 1.5
- first_shift: bfloat16 [768], replicated, may hold values from -3 to 3
- second_gain: bfloat16 [768], replicated, may hold values from 0.5 to 1.5
- second_shift: bfloat16 [768], replicated, may hold values from -3 to 3
- output_grad: bfloat16 [16384, 768], P(('dp', 'mp')), may hold values from -6 to 6
Outputs:
- activations: bfloat16 [16384, 768], P(('dp', 'mp'))
- input_grad: bfloat16 [16384, 768], P(('dp', 'mp'))
- mixer_down_grad: float32 [768, 64], replicated
- mixer_down_bias_grad: float32 [64], replicated
- mixer_up_grad: float32 [64, 768], replicated
- mixer_up_bias_grad: float32 [768], replicated
- dense_down_grad: float32 [768, 64], replicated
- dense_down_bias_grad: float32 [64], replicated
- dense_up_grad: float32 [64, 768], replicated
- dense_up_bias_grad: float32 [768], replicated
- first_gain_grad: float32 [768], replicated
- first_shift_grad: float32 [768], replicated
- second_gain_grad: float32 [768], replicated
- second_shift_grad: float32 [768], replicated
- norm_ratios: float32 [2], replicated
Inputs may be any that keep to these rules, and one draw needn't show every extreme that they name: `segment_ids`: each row numbers the items of one packed batch from 0, never falling.
All inputs are finite; a program needn't handle non-finite values.
Results may differ from a plain program's by a relative error of at most 0.019.
Values may be sent and summed in bfloat16 or wider, within the bound.
No kernel may reach another device: no remote copies, remote signals or barrier semaphores. Data moves between devices by JAX's collectives and lax.ppermute only.
A program may use at most 128 MiB of HBM per device.

v0:
```python
import jax
import jax.numpy as jnp
from jax import lax
from jax.sharding import PartitionSpec as P

HEAD_DIM = 64
EPS = 1e-12
block_limit = 512


def gelu_value(values):
    return jax.nn.gelu(values, approximate=False)


def gelu_slope(values):
    return (
        0.5 * (1.0 + jax.scipy.special.erf(values * 0.7071067811865476))
        + values * jnp.exp(-0.5 * values * values) * 0.3989422804014327
    )


def times_transpose(left, right):
    return lax.dot_general(
        left, right, (((1,), (1,)), ((), ())), preferred_element_type=jnp.float32
    )


def contract_rows(left, right):
    return lax.dot_general(
        left, right, (((0,), (0,)), ((), ())), preferred_element_type=jnp.float32
    )


def norm_forward(residual, gain, shift):
    mean = jnp.mean(residual, -1, keepdims=True)
    centred = residual - mean
    reciprocal = lax.rsqrt(jnp.mean(centred * centred, -1, keepdims=True) + EPS)
    normed = centred * reciprocal
    return (normed * gain + shift, normed, reciprocal)


def norm_backward(upstream, normed, reciprocal, gain):
    scaled = upstream * gain
    inflow = reciprocal * (
        scaled
        - jnp.mean(scaled, -1, keepdims=True)
        - normed * jnp.mean(scaled * normed, -1, keepdims=True)
    )
    return (inflow, jnp.sum(upstream * normed, 0), jnp.sum(upstream, 0))


def adapter_forward(inflow, down, down_bias, up, up_bias):
    inflow_low = inflow.astype(jnp.bfloat16)
    inner = jnp.dot(inflow_low, down, preferred_element_type=jnp.float32) + down_bias.astype(
        jnp.float32
    )
    active = gelu_value(inner).astype(jnp.bfloat16)
    outflow = jnp.dot(active, up, preferred_element_type=jnp.float32) + up_bias.astype(jnp.float32)
    return (outflow, (inflow_low, inner, active))


def adapter_backward(grad_out, kept, down, up):
    inflow_low, inner, active = kept
    grad_top = grad_out.astype(jnp.bfloat16)
    up_grad = contract_rows(active, grad_top)
    up_bias_grad = jnp.sum(grad_top.astype(jnp.float32), 0)
    grad_mid = (times_transpose(grad_top, up) * gelu_slope(inner)).astype(jnp.bfloat16)
    down_grad = contract_rows(inflow_low, grad_mid)
    down_bias_grad = jnp.sum(grad_mid.astype(jnp.float32), 0)
    inflow_grad = times_transpose(grad_mid, down)
    return (inflow_grad, (down_grad, down_bias_grad, up_grad, up_bias_grad))


def score_block(query_rows, query_seg, keys, key_seg, scale):
    scores = (
        jnp.einsum("qhd,khd->hqk", query_rows, keys, preferred_element_type=jnp.float32) * scale
    )
    same = query_seg[:, None] == key_seg[None, :]
    return jnp.where(same[None], scores, -1e30)


def attention_forward(queries, keys, values, seg_row, block, scale):
    count = queries.shape[0] // block

    def one_block(index):
        start = index * block
        rows = lax.dynamic_slice_in_dim(queries, start, block, 0)
        row_seg = lax.dynamic_slice_in_dim(seg_row, start, block, 0)
        scores = score_block(rows, row_seg, keys, seg_row, scale)
        peak = jnp.max(scores, -1, keepdims=True)
        exponent = jnp.exp(scores - peak)
        total = jnp.sum(exponent, -1, keepdims=True)
        shares = (exponent / total).astype(jnp.bfloat16)
        mixed = jnp.einsum("hqk,khd->qhd", shares, values, preferred_element_type=jnp.float32)
        return (mixed.astype(jnp.bfloat16), (peak + jnp.log(total))[..., 0])

    mixed, log_totals = lax.map(one_block, jnp.arange(count))
    return (mixed.reshape(queries.shape), log_totals)


def attention_backward(queries, keys, values, seg_row, log_totals, mixed_grad, block, scale):
    count = queries.shape[0] // block

    def one_block(carry, index):
        key_grad, value_grad = carry
        start = index * block
        rows = lax.dynamic_slice_in_dim(queries, start, block, 0)
        row_seg = lax.dynamic_slice_in_dim(seg_row, start, block, 0)
        grad_rows = lax.dynamic_slice_in_dim(mixed_grad, start, block, 0)
        scores = score_block(rows, row_seg, keys, seg_row, scale)
        shares = jnp.exp(scores - log_totals[index][..., None])
        value_grad = value_grad + jnp.einsum(
            "hqk,qhd->khd",
            shares.astype(jnp.bfloat16),
            grad_rows,
            preferred_element_type=jnp.float32,
        )
        share_grad = jnp.einsum(
            "qhd,khd->hqk", grad_rows, values, preferred_element_type=jnp.float32
        )
        score_grad = (
            shares * (share_grad - jnp.sum(shares * share_grad, -1, keepdims=True))
        ).astype(jnp.bfloat16)
        query_grad = (
            jnp.einsum("hqk,khd->qhd", score_grad, keys, preferred_element_type=jnp.float32) * scale
        ).astype(jnp.bfloat16)
        key_grad = (
            key_grad
            + jnp.einsum("hqk,qhd->khd", score_grad, rows, preferred_element_type=jnp.float32)
            * scale
        )
        return ((key_grad, value_grad), query_grad)

    zeros = jnp.zeros(keys.shape, jnp.float32)
    (key_grad, value_grad), query_grad = lax.scan(one_block, (zeros, zeros), jnp.arange(count))
    return (
        query_grad.reshape(queries.shape),
        key_grad.astype(jnp.bfloat16),
        value_grad.astype(jnp.bfloat16),
    )


def per_device(
    tokens,
    segment_ids,
    query_weight,
    key_weight,
    value_weight,
    output_weight,
    inner_weight,
    outer_weight,
    mixer_down,
    mixer_down_bias,
    mixer_up,
    mixer_up_bias,
    dense_down,
    dense_down_bias,
    dense_up,
    dense_up_bias,
    first_gain,
    first_shift,
    second_gain,
    second_shift,
    output_grad,
):
    shard_rows = tokens.shape[0]
    group_rows = shard_rows * lax.axis_size("mp")
    seg_row = segment_ids[0]
    block = min(block_limit, group_rows)
    scale = HEAD_DIM ** (-0.5)
    width = query_weight.shape[1]
    local_heads = width // HEAD_DIM
    head_shape = (group_rows, local_heads, HEAD_DIM)
    gain_one = first_gain.astype(jnp.float32)
    gain_two = second_gain.astype(jnp.float32)
    piece = lax.all_gather(tokens, "mp", axis=0, tiled=True)
    projected = jnp.concatenate(
        [
            jnp.dot(piece, query_weight, preferred_element_type=jnp.float32).astype(jnp.bfloat16),
            jnp.dot(piece, key_weight, preferred_element_type=jnp.float32).astype(jnp.bfloat16),
            jnp.dot(piece, value_weight, preferred_element_type=jnp.float32).astype(jnp.bfloat16),
        ],
        1,
    )
    queries = projected[:, :width].reshape(head_shape)
    keys = projected[:, width : 2 * width].reshape(head_shape)
    values = projected[:, 2 * width :].reshape(head_shape)
    mixed, log_totals = attention_forward(queries, keys, values, seg_row, block, scale)
    mixed_flat = mixed.reshape(group_rows, width)
    attended = lax.psum_scatter(
        jnp.dot(mixed_flat, output_weight, preferred_element_type=jnp.float32),
        "mp",
        scatter_dimension=0,
        tiled=True,
    )
    token_values = tokens.astype(jnp.float32)
    mixer_out, mixer_kept = adapter_forward(
        attended, mixer_down, mixer_down_bias, mixer_up, mixer_up_bias
    )
    hidden, normed_one, recip_one = norm_forward(
        token_values + attended + mixer_out, gain_one, first_shift.astype(jnp.float32)
    )
    hidden_low = hidden.astype(jnp.bfloat16)
    inner = jnp.dot(
        lax.all_gather(hidden_low, "mp", axis=0, tiled=True),
        inner_weight,
        preferred_element_type=jnp.float32,
    )
    inner_low = gelu_value(inner).astype(jnp.bfloat16)
    dense_in = lax.psum_scatter(
        jnp.dot(inner_low, outer_weight, preferred_element_type=jnp.float32).astype(jnp.bfloat16),
        "mp",
        scatter_dimension=0,
        tiled=True,
    ).astype(jnp.float32)
    dense_out, dense_kept = adapter_forward(
        dense_in, dense_down, dense_down_bias, dense_up, dense_up_bias
    )
    result, normed_two, recip_two = norm_forward(
        hidden + dense_in + dense_out, gain_two, second_shift.astype(jnp.float32)
    )
    mixer_square = jnp.sum(mixer_out * mixer_out)
    dense_square = jnp.sum(dense_out * dense_out)
    input_square = jnp.sum(token_values * token_values)
    mixer_square, dense_square, input_square = lax.psum(
        (mixer_square, dense_square, input_square), ("dp", "mp")
    )
    upstream = output_grad.astype(jnp.float32)
    second_grad, second_gain_grad, second_shift_grad = norm_backward(
        upstream, normed_two, recip_two, gain_two
    )
    dense_back, dense_grads = adapter_backward(second_grad, dense_kept, dense_down, dense_up)
    dense_in_grad = (second_grad + dense_back).astype(jnp.bfloat16)
    inner_full = times_transpose(
        lax.all_gather(dense_in_grad, "mp", axis=0, tiled=True), outer_weight
    )
    inner_grad = (inner_full * gelu_slope(inner)).astype(jnp.bfloat16)
    hidden_back = lax.psum_scatter(
        times_transpose(inner_grad, inner_weight).astype(jnp.bfloat16),
        "mp",
        scatter_dimension=0,
        tiled=True,
    ).astype(jnp.float32)
    hidden_grad = second_grad + hidden_back
    first_grad, first_gain_grad, first_shift_grad = norm_backward(
        hidden_grad, normed_one, recip_one, gain_one
    )
    mixer_back, mixer_grads = adapter_backward(first_grad, mixer_kept, mixer_down, mixer_up)
    attended_grad = (first_grad + mixer_back).astype(jnp.bfloat16)
    mixed_grad = (
        times_transpose(lax.all_gather(attended_grad, "mp", axis=0, tiled=True), output_weight)
        .astype(jnp.bfloat16)
        .reshape(head_shape)
    )
    query_grad, key_grad, value_grad = attention_backward(
        queries, keys, values, seg_row, log_totals, mixed_grad, block, scale
    )
    query_flat = query_grad.reshape(group_rows, width)
    key_flat = key_grad.reshape(group_rows, width)
    value_flat = value_grad.reshape(group_rows, width)
    total = times_transpose(query_flat, query_weight)
    total = total + times_transpose(key_flat, key_weight)
    input_back = lax.psum_scatter(
        (total + times_transpose(value_flat, value_weight)).astype(jnp.bfloat16),
        "mp",
        scatter_dimension=0,
        tiled=True,
    ).astype(jnp.float32)
    input_grad = (first_grad + input_back).astype(jnp.bfloat16)
    summed = lax.psum(
        (
            mixer_grads[0],
            mixer_grads[1],
            mixer_grads[2],
            mixer_grads[3],
            dense_grads[0],
            dense_grads[1],
            dense_grads[2],
            dense_grads[3],
            first_gain_grad,
            first_shift_grad,
            second_gain_grad,
            second_shift_grad,
        ),
        ("dp", "mp"),
    )
    ratios = jnp.sqrt(jnp.stack([mixer_square, dense_square]) / input_square)
    return (
        result.astype(jnp.bfloat16),
        input_grad,
        summed[0],
        summed[1],
        summed[2],
        summed[3],
        summed[4],
        summed[5],
        summed[6],
        summed[7],
        summed[8],
        summed[9],
        summed[10],
        summed[11],
        ratios,
    )


def solution(mesh):
    placed = (
        P(("dp", "mp"), None),
        P("dp", None),
        P(None, "mp"),
        P(None, "mp"),
        P(None, "mp"),
        P("mp", None),
        P(None, "mp"),
        P("mp", None),
        P(),
        P(),
        P(),
        P(),
        P(),
        P(),
        P(),
        P(),
        P(),
        P(),
        P(),
        P(),
        P(("dp", "mp"), None),
    )
    return jax.shard_map(
        per_device,
        mesh=mesh,
        in_specs=placed,
        out_specs=(
            P(("dp", "mp"), None),
            P(("dp", "mp"), None),
            P(),
            P(),
            P(),
            P(),
            P(),
            P(),
            P(),
            P(),
            P(),
            P(),
            P(),
            P(),
            P(),
        ),
        check_vma=False,
    )
```

profile of v0, /device:TPU:0, one launch (start us, length us, event | category | flops | bytes accessed | tf_op | source)
XLA Modules:
  0.0 461.6 jit_solution(3610006697994505217)
XLA Ops:
  8.0 14.1 %all-gather.5.cloned.1.call-done = bf16[1024,768]{1,0:T(8,128)(2,1)} async-done(((bf16[512,768]{1,0:T(8,128)(2,1)}), bf16[1024,768]{1,0:T(8,128)(2,1)}) %all-gather.5.cloned.1.call-update) | async-done | bytes 1572880 | tf_op jit(solution)/shard_map/all_gather | solution.py:176
  22.1 3.4 convolution_convert_fusion.4
  26.4 1.7 convolution_convert_fusion.2
  29.1 27.5 %while.27 = (s32[]{:T(128)}, bf16[2,512,6,64]{1,3,2,0:T(8,128)(2,1)}, f32[2,6,512]{2,1,0:T(8,128)S(1)}, s32[2]{0:T(128)S(1)}, s32[1024]{0:T(1024)S(1)}, /*index=...) while((s32[]{:T(128)}, ...), condition=%wide.region_3.4_spmd, body=%wide.region_0.3_spmd.sunk | while | flops 843772928 | bytes 45472476 | solution.py:97
  30.7 3.4 fusion.212
  34.1 3.6 fusion.213
  37.8 5.0 %fusion.214 = bf16[2,512,6,64]{1,3,2,0:T(8,128)(2,1)} fusion(bf16[2,512,6,64]{1,3,2,0:T(8,128)(2,1)} %get-tuple-element.408, s32[]{:T(128)} %get-tuple-element.407, bf16[1024,6,64]{0,2,1:T(8,128)(2,1)S(1)} %copy-done.10, f32[6,512,1024]{2,1,0:T(8,128)S(1)} %get-tuple-element.378, f32[6,512]{1,0:T(8,128)S(1)} %fusion.213, ...), kind=kOutput, calls=%fused_computation.8.clone.1 | convolution fusion | flops 418578432 | bytes 14311936 | tf_op jit(solution)/shard_map/while/body/eval_jaxpr/hqk,khd->qhd/dot_general | solution.py:94
  44.5 3.4 fusion.212
  47.9 3.6 fusion.213
  51.5 5.0 %fusion.214 = bf16[2,512,6,64]{1,3,2,0:T(8,128)(2,1)} fusion(bf16[2,512,6,64]{1,3,2,0:T(8,128)(2,1)} %get-tuple-element.408, s32[]{:T(128)} %get-tuple-element.407, bf16[1024,6,64]{0,2,1:T(8,128)(2,1)S(1)} %copy-done.10, f32[6,512,1024]{2,1,0:T(8,128)S(1)} %get-tuple-element.378, f32[6,512]{1,0:T(8,128)S(1)} %fusion.213, ...), kind=kOutput, calls=%fused_computation.8.clone.1 | convolution fusion | flops 418578432 | bytes 14311936 | tf_op jit(solution)/shard_map/while/body/eval_jaxpr/hqk,khd->qhd/dot_general | solution.py:94
  56.5 2.0 copy.36
  58.7 2.7 fusion.146
  61.6 12.1 %reduce-scatter.5.cloned.1.call-done = f32[512,768]{1,0:T(8,128)} async-done(((f32[1024,768]{1,0:T(8,128)}), f32[512,768]{1,0:T(8,128)}) %reduce-scatter.5.cloned.1.call-update) | async-done | bytes 1572880 | tf_op jit(solution)/shard_map/reduce_scatter | solution.py:190
  73.7 1.8 convolution_add_fusion.3
  75.5 3.2 fusion.144
  81.6 10.6 %all-gather.7.cloned.1.call-done = bf16[1024,768]{1,0:T(8,128)(2,1)} async-done(((bf16[512,768]{1,0:T(8,128)(2,1)}), bf16[1024,768]{1,0:T(8,128)(2,1)}) %all-gather.7.cloned.1.call-update) | async-done | bytes 1572880 | tf_op jit(solution)/shard_map/all_gather | solution.py:205
  92.2 4.2 fusion.147
  96.3 2.6 copy-done.56
  99.0 17.3 %fusion.53 = bf16[1024,768]{1,0:T(8,128)(2,1)} fusion(bf16[1536,768]{1,0:T(8,128)(2,1)S(1)} %copy-done.52, f32[1024,1536]{1,0:T(8,128)S(1)} %fusion.147), kind=kOutput, calls=%fused_computation.78 | convolution fusion | flops 2518941696 | bytes 10223616 | tf_op jit(solution)/shard_map/dot_general | solution.py:211
  116.5 10.3 %reduce-scatter.7.cloned.1.call-done = bf16[512,768]{1,0:T(8,128)(2,1)} async-done(((bf16[1024,768]{1,0:T(8,128)(2,1)}), bf16[512,768]{1,0:T(8,128)(2,1)}) %reduce-scatter.7.cloned.1.call-update) | async-done | bytes 786448 | tf_op jit(solution)/shard_map/reduce_scatter | solution.py:210
  128.3 3.5 fusion.143
  138.0 11.1 %all-gather.9.cloned.1.call-done = bf16[1024,768]{1,0:T(8,128)(2,1)} async-done(((bf16[512,768]{1,0:T(8,128)(2,1)}), bf16[1024,768]{1,0:T(8,128)(2,1)}) %all-gather.9.cloned.1.call-update) | async-done | bytes 1572880 | tf_op jit(solution)/shard_map/all_gather | solution.py:235
  149.1 10.5 %convolution_convert_fusion = bf16[1024,768]{1,0:T(8,128)(2,1)} fusion(bf16[768,1536]{1,0:T(8,128)(2,1)S(1)} %copy-done, f32[1024,1536]{1,0:T(8,128)} %copy-done.56, bf16[1024,768]{1,0:T(8,128)(2,1)} %all-gather.9.cloned.1.call-done, bf16[1536,768]{1,0:T(8,128)(2,1)} %param.32), kind=kOutput, calls=%fused_computation.79 | convolution fusion | flops 4848353280 | bytes 14155776 | tf_op jit(solution)/shard_map/dot_general | solution.py:23
  159.8 10.2 %reduce-scatter.9.cloned.1.call-done = bf16[512,768]{1,0:T(8,128)(2,1)} async-done(((bf16[1024,768]{1,0:T(8,128)(2,1)}), bf16[512,768]{1,0:T(8,128)(2,1)}) %reduce-scatter.9.cloned.1.call-update) | async-done | bytes 786448 | tf_op jit(solution)/shard_map/reduce_scatter | solution.py:238
  169.9 4.1 multiply_reduce_fusion.3
  177.8 11.1 %all-gather.11.cloned.1.call-done = bf16[1024,768]{1,0:T(8,128)(2,1)} async-done(((bf16[512,768]{1,0:T(8,128)(2,1)}), bf16[1024,768]{1,0:T(8,128)(2,1)}) %all-gather.11.cloned.1.call-update) | async-done | bytes 1572880 | tf_op jit(solution)/shard_map/all_gather | solution.py:251
  188.9 3.1 convolution_convert_fusion.1
  192.9 98.8 %while.28 = (s32[]{:T(128)}, f32[1024,6,64]{0,2,1:T(8,128)S(1)}, f32[1024,6,64]{0,2,1:T(8,128)}, bf16[2,512,6,64]{1,3,2,0:T(8,128)(2,1)}, s32[2]{0:T(128)S(1)}, ...) while((s32[]{:T(128)}, f32[1024,6,64]{0,2,1:T(8,128)S(1)}, ...), condition=%wide.region_17.18_spmd.clone, body=%wide.region_15.17_spmd.clone.sunk | while | flops 2063332352 | bytes 179538384 | solution.py:135
  194.2 7.4 %fusion.224 = f32[6,512,1024]{2,1,0:T(8,128)} fusion(bf16[1024,6,64]{0,2,1:T(8,128)(2,1)S(1)} %get-tuple-element.475, bf16[1024,6,64]{0,2,1:T(8,128)(2,1)} %get-tuple-element.472, s32[]{:T(128)S(6)} %select_n.64), kind=kOutput, calls=%fused_computation.33.clone.1 | convolution fusion | flops 402653184 | bytes 13762564 | tf_op jit(solution)/shard_map/while/body/eval_jaxpr/qhd,khd->hqk/dot_general | solution.py:76
  204.0 11.6 %multiply_reduce_fusion.9 = (f32[6,512]{1,0:T(8,128)S(1)}, f32[6,512,1024]{2,1,0:T(8,128)}) fusion(f32[6,512,1024]{2,1,0:T(8,128)} %fusion.224, f32[6,512]{1,0:T(8,128)S(1)} %dynamic-slice_bitcast_fusion.2, pred[512,1024]{1,0:T(8,128)(4,1)S(1)} %broadcast_compare_fusion.5, bf16[1024,6,64]{0,2,1:T(8,128)(2,1)} %get-tuple-element.478, ...), kind=kOutput, calls=%fused_computation.17.clone.1 | convolution fusion | flops 418378752 | bytes 26894340 | tf_op jit(solution)/shard_map/while/body/eval_jaxpr/qhd,khd->hqk/dot_general | solution.py:118
  216.9 9.6 %multiply_convert_fusion.2 = bf16[6,512,1024]{2,1,0:T(8,128)(2,1)} fusion(f32[6,512,1024]{2,1,0:T(8,128)} %get-tuple-element.392, f32[6,512,1024]{2,1,0:T(8,128)S(1)} %bitcast.121, f32[6,512]{1,0:T(8,128)S(1)} %get-tuple-element.393, f32[6,512]{1,0:T(8,128)S(1)} %dynamic-slice_bitcast_fusion.2, pred[512,1024]{1,0:T(8,128)(4,1)S(1)} %broadcast_compare_fusion.5), kind=kLoop, calls=%fused_computation.16.clone.1 | loop fusion | flops 18874368 | bytes 32006144 | tf_op jit(solution)/shard_map/while/body/eval_jaxpr/convert_element_type | solution.py:123
  226.6 4.4 bitcast_add_fusion.4
  231.4 2.0 fusion.225
  234.3 7.7 %bitcast_add_fusion.5 = f32[1024,6,64]{0,2,1:T(8,128)} fusion(f32[1024,6,64]{0,2,1:T(8,128)} %get-tuple-element.452, f32[6,512,1024]{2,1,0:T(8,128)} %fusion.224, f32[6,512]{1,0:T(8,128)S(1)} %dynamic-slice_bitcast_fusion.2, pred[512,1024]{1,0:T(8,128)(4,1)S(1)} %broadcast_compare_fusion.5, pred[]{:T(512)S(6)} %compare.3, ...), kind=kOutput, calls=%fused_computation.22.clone.1 | convolution fusion | flops 416022528 | bytes 16662533 | tf_op jit(solution)/shard_map/while/body/eval_jaxpr/hqk,qhd->khd/dot_general | solution.py:112
  243.3 7.4 %fusion.224 = f32[6,512,1024]{2,1,0:T(8,128)} fusion(bf16[1024,6,64]{0,2,1:T(8,128)(2,1)S(1)} %get-tuple-element.475, bf16[1024,6,64]{0,2,1:T(8,128)(2,1)} %get-tuple-element.472, s32[]{:T(128)S(6)} %select_n.64), kind=kOutput, calls=%fused_computation.33.clone.1 | convolution fusion | flops 402653184 | bytes 13762564 | tf_op jit(solution)/shard_map/while/body/eval_jaxpr/qhd,khd->hqk/dot_general | solution.py:76
  253.1 11.6 %multiply_reduce_fusion.9 = (f32[6,512]{1,0:T(8,128)S(1)}, f32[6,512,1024]{2,1,0:T(8,128)}) fusion(f32[6,512,1024]{2,1,0:T(8,128)} %fusion.224, f32[6,512]{1,0:T(8,128)S(1)} %dynamic-slice_bitcast_fusion.2, pred[512,1024]{1,0:T(8,128)(4,1)S(1)} %broadcast_compare_fusion.5, bf16[1024,6,64]{0,2,1:T(8,128)(2,1)} %get-tuple-element.478, ...), kind=kOutput, calls=%fused_computation.17.clone.1 | convolution fusion | flops 418378752 | bytes 26894340 | tf_op jit(solution)/shard_map/while/body/eval_jaxpr/qhd,khd->hqk/dot_general | solution.py:118
  266.0 9.6 %multiply_convert_fusion.2 = bf16[6,512,1024]{2,1,0:T(8,128)(2,1)} fusion(f32[6,512,1024]{2,1,0:T(8,128)} %get-tuple-element.392, f32[6,512,1024]{2,1,0:T(8,128)S(1)} %bitcast.121, f32[6,512]{1,0:T(8,128)S(1)} %get-tuple-element.393, f32[6,512]{1,0:T(8,128)S(1)} %dynamic-slice_bitcast_fusion.2, pred[512,1024]{1,0:T(8,128)(4,1)S(1)} %broadcast_compare_fusion.5), kind=kLoop, calls=%fused_computation.16.clone.1 | loop fusion | flops 18874368 | bytes 32006144 | tf_op jit(solution)/shard_map/while/body/eval_jaxpr/convert_element_type | solution.py:123
  275.7 4.4 bitcast_add_fusion.4
  280.5 2.0 fusion.225
  283.4 8.1 %bitcast_add_fusion.5 = f32[1024,6,64]{0,2,1:T(8,128)} fusion(f32[1024,6,64]{0,2,1:T(8,128)} %get-tuple-element.452, f32[6,512,1024]{2,1,0:T(8,128)} %fusion.224, f32[6,512]{1,0:T(8,128)S(1)} %dynamic-slice_bitcast_fusion.2, pred[512,1024]{1,0:T(8,128)(4,1)S(1)} %broadcast_compare_fusion.5, pred[]{:T(512)S(6)} %compare.3, ...), kind=kOutput, calls=%fused_computation.22.clone.1 | convolution fusion | flops 416022528 | bytes 16662533 | tf_op jit(solution)/shard_map/while/body/eval_jaxpr/hqk,qhd->khd/dot_general | solution.py:112
  291.8 2.0 copy.37
  297.7 2.2 add_convert_fusion
  300.0 2.2 fusion.150
  305.7 41.6 %all-reduce = (f32[64]{0:T(128)}, f32[768]{0:T(1024)}, f32[64]{0:T(128)}, f32[768]{0:T(1024)}, f32[768]{0:T(1024)}, /*index=5*/f32[768]{0:T(1024)}, f32[768]{0:T...) all-reduce(f32[64]{0:T(128)S(1)} %copy-done.51, ...), channel_id=1, replica_groups=mesh['dp'=16,'mp'=2] {'dp','mp'}, use_global_device_ids=true, to_apply=%region_21.22 | all-reduce | flops 4739 | bytes 37912 | tf_op jit(solution)/shard_map/psum | solution.py:270
  347.3 2.5 fusion.96
  349.8 2.6 add_convert_fusion.1
  352.4 96.0 %all-reduce.4.cloned.1.call-done = (f32[768,64]{0,1:T(8,128)}, f32[64,768]{1,0:T(8,128)}, f32[768,64]{0,1:T(8,128)}, f32[64,768]{1,0:T(8,128)}) async-done(((f32[768,64]{0,1:T(8,128)}, f32[64,768]{1,0:T(8,128)}, f32[768,64]{0,1:T(8,128)}, f32[64,768]{1,0:T(8,128)}), (f32[768,64]{0,1:T(8,128)}, f32[64,768]{1,0:T(8,128)}, f32[768,64]{0,1:T(8,128)}, f32[64,768]{1,0:T(8,128)})) %all-reduce.4.cloned.1.call-update) | async-done | bytes 786448 | tf_op jit(solution)/shard_map/psum | solution.py:270
  448.4 1.6 copy.68
  (218 shorter events, 39.9 us)
Async XLA Ops:
  7.2 85.0 %copy-start = (bf16[768,1536]{1,0:T(8,128)(2,1)S(1)}, bf16[768,1536]{1,0:T(8,128)(2,1)}, u32[]{:S(2)}) copy-start(bf16[768,1536]{1,0:T(8,128)(2,1)} %param.31) | copy-start | bytes 7077892
  7.2 14.9 %all-gather.5.cloned.1.call-start = ((), (), s32[]{:S(2)}) async-start(), calls=%async_computation.4 | async-start | bytes 2359296 | tf_op jit(solution)/shard_map/all_gather | solution.py:176
  7.9 65.7 %reduce-scatter.5.cloned.1.call-start = ((), (), s32[]{:S(2)}) async-start(), calls=%async_computation.5 | async-start | bytes 4718592 | tf_op jit(solution)/shard_map/reduce_scatter | solution.py:190
  22.1 3.4 copy-start.21
  22.1 3.4 copy-start.53
  22.1 4.3 copy-start.23
  34.1 3.7 copy-start.10
  47.9 3.7 copy-start.10
  58.7 14.9 %copy-start.34 = (bf16[768,64]{0,1:T(8,128)(2,1)S(1)}, bf16[768,64]{0,1:T(8,128)(2,1)}, u32[]{:S(2)}) copy-start(bf16[768,64]{0,1:T(8,128)(2,1)} %param.33) | copy-start | bytes 294916
  61.4 14.0 %copy-start.36 = (bf16[64,768]{1,0:T(8,128)(2,1)S(1)}, bf16[64,768]{1,0:T(8,128)(2,1)}, u32[]{:S(2)}) copy-start(bf16[64,768]{1,0:T(8,128)(2,1)} %param.35) | copy-start | bytes 294916
  61.4 30.7 %all-gather.7.cloned.1.call-start = ((), (), s32[]{:S(2)}) async-start(), calls=%async_computation.6 | async-start | bytes 2359296 | tf_op jit(solution)/shard_map/all_gather | solution.py:205
  75.4 99.8 %copy-start.31 = (f32[512,64]{0,1:T(8,128)}, f32[512,64]{0,1:T(8,128)S(1)}, u32[]{:S(2)}) copy-start(f32[512,64]{0,1:T(8,128)S(1)} %convolution_add_fusion.3) | copy-start | bytes 393220
  81.0 45.7 %reduce-scatter.7.cloned.1.call-start = ((), (), s32[]{:S(2)}) async-start(), calls=%async_computation.7 | async-start | bytes 2359296 | tf_op jit(solution)/shard_map/reduce_scatter | solution.py:210
  92.2 6.8 %copy-start.52 = (bf16[1536,768]{1,0:T(8,128)(2,1)S(1)}, bf16[1536,768]{1,0:T(8,128)(2,1)}, u32[]{:S(2)}) copy-start(bf16[1536,768]{1,0:T(8,128)(2,1)} %param.32) | copy-start | bytes 7077892
  99.0 17.4 %copy-start.55 = (bf16[64]{0:T(256)(128)(2,1)S(1)}, bf16[64]{0:T(256)(128)(2,1)}, u32[]{:S(2)}) copy-start(bf16[64]{0:T(256)(128)(2,1)} %param.38) | copy-start | bytes 388
  99.0 17.5 %copy-start.47 = (bf16[768]{0:T(1024)(128)(2,1)S(1)}, bf16[768]{0:T(1024)(128)(2,1)}, u32[]{:S(2)}) copy-start(bf16[768]{0:T(1024)(128)(2,1)} %param.40) | copy-start | bytes 4612
  99.0 17.5 %copy-start.48 = (bf16[768]{0:T(1024)(128)(2,1)S(1)}, bf16[768]{0:T(1024)(128)(2,1)}, u32[]{:S(2)}) copy-start(bf16[768]{0:T(1024)(128)(2,1)} %param.43) | copy-start | bytes 4612
  99.0 17.5 %copy-start.49 = (bf16[768]{0:T(1024)(128)(2,1)S(1)}, bf16[768]{0:T(1024)(128)(2,1)}, u32[]{:S(2)}) copy-start(bf16[768]{0:T(1024)(128)(2,1)} %param.44) | copy-start | bytes 4612
  99.0 27.8 %copy-start.33 = (bf16[768,64]{0,1:T(8,128)(2,1)S(1)}, bf16[768,64]{0,1:T(8,128)(2,1)}, u32[]{:S(2)}) copy-start(bf16[768,64]{0,1:T(8,128)(2,1)} %param.37) | copy-start | bytes 294916
  116.4 32.7 %all-gather.9.cloned.1.call-start = ((), (), s32[]{:S(2)}) async-start(), calls=%async_computation.8 | async-start | bytes 2359296 | tf_op jit(solution)/shard_map/all_gather | solution.py:235
  128.3 6.7 %copy-start.29 = (f32[512,64]{0,1:T(8,128)}, f32[512,64]{0,1:T(8,128)S(1)}, u32[]{:S(2)}) copy-start(f32[512,64]{0,1:T(8,128)S(1)} %convolution_add_fusion.2) | copy-start | bytes 393220
  128.3 3.8 copy-start.13
  137.9 32.0 %reduce-scatter.9.cloned.1.call-start = ((), (), s32[]{:S(2)}) async-start(), calls=%async_computation.9 | async-start | bytes 2359296 | tf_op jit(solution)/shard_map/reduce_scatter | solution.py:238
  159.5 14.5 %copy-start.4 = (f32[512,768]{1,0:T(8,128)S(1)}, f32[512,768]{1,0:T(8,128)}, u32[]{:S(2)}) copy-start(f32[512,768]{1,0:T(8,128)} %copy-done.3) | copy-start | bytes 4718596
  159.5 29.3 %all-gather.11.cloned.1.call-start = ((), (), s32[]{:S(2)}) async-start(), calls=%async_computation.10 | async-start | bytes 2359296 | tf_op jit(solution)/shard_map/all_gather | solution.py:251
  169.9 4.1 copy-start.9
  169.9 4.1 copy-start.16
  175.3 13.6 %copy-start.19 = (bf16[384,768]{1,0:T(8,128)(2,1)S(1)}, bf16[384,768]{1,0:T(8,128)(2,1)}, u32[]{:S(2)}) copy-start(bf16[384,768]{1,0:T(8,128)(2,1)} %param.30) | copy-start | bytes 1769476
  176.2 15.7 %copy-start.27 = (bf16[512,64]{0,1:T(8,128)(2,1)}, bf16[512,64]{0,1:T(8,128)(2,1)S(1)}, u32[]{:S(2)}) copy-start(bf16[512,64]{0,1:T(8,128)(2,1)S(1)} %get-tuple-element.253) | copy-start | bytes 196612
  177.7 172.1 %reduce-scatter.11.cloned.1.call-start = ((), (), s32[]{:S(2)}) async-start(), calls=%async_computation.11 | async-start | bytes 2359296 | tf_op jit(solution)/shard_map/reduce_scatter | solution.py:263
  203.9 11.7 %slice-start = ((s8[12582912]{0:T(1024)(128)(4,1)}), s8[4194304]{0:T(1024)(128)(4,1)S(1)}, s32[]{:S(2)}) async-start(s8[12582912]{0:T(1024)(128)(4,1)} %bitcast.120), calls=%async_computation.13 | async-start | bytes 8388608 | tf_op jit(solution)/shard_map/while
  203.9 11.7 %slice-start.1 = ((s8[12582912]{0:T(1024)(128)(4,1)}), s8[4194304]{0:T(1024)(128)(4,1)S(1)}, s32[]{:S(2)}) async-start(s8[12582912]{0:T(1024)(128)(4,1)} %bitcast.120), calls=%async_computation.14 | async-start | bytes 8388608 | tf_op jit(solution)/shard_map/while
  204.0 13.0 %slice-start.2 = ((s8[12582912]{0:T(1024)(128)(4,1)}), s8[4194304]{0:T(1024)(128)(4,1)S(1)}, s32[]{:S(2)}) async-start(s8[12582912]{0:T(1024)(128)(4,1)} %bitcast.120), calls=%async_computation.15 | async-start | bytes 8388608 | tf_op jit(solution)/shard_map/while
  226.6 4.7 %copy-start.2 = (bf16[6,512,1024]{2,1,0:T(8,128)(2,1)S(1)}, bf16[6,512,1024]{2,1,0:T(8,128)(2,1)}, u32[]{:S(2)}) copy-start(bf16[6,512,1024]{2,1,0:T(8,128)(2,1)} %multiply_convert_fusion.2) | copy-start | bytes 18874372 | tf_op jit(solution)/shard_map/while
  226.6 4.9 %copy-start.14 = (bf16[2,512,6,64]{1,3,2,0:T(8,128)(2,1)S(1)}, bf16[2,512,6,64]{1,3,2,0:T(8,128)(2,1)}, u32[]{:S(2)}) copy-start(bf16[2,512,6,64]{1,3,2,0:T(8,128)(2,1)} %get-tuple-element.453) | copy-start | bytes 2359300 | tf_op jit(solution)/shard_map/while
  253.0 11.7 %slice-start = ((s8[12582912]{0:T(1024)(128)(4,1)}), s8[4194304]{0:T(1024)(128)(4,1)S(1)}, s32[]{:S(2)}) async-start(s8[12582912]{0:T(1024)(128)(4,1)} %bitcast.120), calls=%async_computation.13 | async-start | bytes 8388608 | tf_op jit(solution)/shard_map/while
  253.0 11.7 %slice-start.1 = ((s8[12582912]{0:T(1024)(128)(4,1)}), s8[4194304]{0:T(1024)(128)(4,1)S(1)}, s32[]{:S(2)}) async-start(s8[12582912]{0:T(1024)(128)(4,1)} %bitcast.120), calls=%async_computation.14 | async-start | bytes 8388608 | tf_op jit(solution)/shard_map/while
  253.0 13.0 %slice-start.2 = ((s8[12582912]{0:T(1024)(128)(4,1)}), s8[4194304]{0:T(1024)(128)(4,1)S(1)}, s32[]{:S(2)}) async-start(s8[12582912]{0:T(1024)(128)(4,1)} %bitcast.120), calls=%async_computation.15 | async-start | bytes 8388608 | tf_op jit(solution)/shard_map/while
  275.6 4.7 %copy-start.2 = (bf16[6,512,1024]{2,1,0:T(8,128)(2,1)S(1)}, bf16[6,512,1024]{2,1,0:T(8,128)(2,1)}, u32[]{:S(2)}) copy-start(bf16[6,512,1024]{2,1,0:T(8,128)(2,1)} %multiply_convert_fusion.2) | copy-start | bytes 18874372 | tf_op jit(solution)/shard_map/while
  275.6 4.9 %copy-start.14 = (bf16[2,512,6,64]{1,3,2,0:T(8,128)(2,1)S(1)}, bf16[2,512,6,64]{1,3,2,0:T(8,128)(2,1)}, u32[]{:S(2)}) copy-start(bf16[2,512,6,64]{1,3,2,0:T(8,128)(2,1)} %get-tuple-element.453) | copy-start | bytes 2359300 | tf_op jit(solution)/shard_map/while
  297.7 4.6 copy-start.5
  297.7 4.6 copy-start.30
  299.9 3.5 copy-start.11
  299.9 3.5 copy-start.28
  299.9 4.5 copy-start.32
  299.9 148.5 %all-reduce.4.cloned.1.call-start = ((), (), s32[]{:S(2)}) async-start(), calls=%async_computation.12 | async-start | bytes 1572864 | tf_op jit(solution)/shard_map/psum | solution.py:270
  300.0 4.4 copy-start.7
  304.4 150.4 %copy-start.1 = (bf16[768,1536]{1,0:T(8,128)(2,1)S(1)}, bf16[768,1536]{1,0:T(8,128)(2,1)}, u32[]{:S(2)}) copy-start(bf16[768,1536]{1,0:T(8,128)(2,1)} %param.31) | copy-start | bytes 7077892
  (29 other events, 60.7 us)
Sparse Core Ops, SparseCore 0:
  9.6 12.4 all-gather.4
  61.6 12.0 reduce-scatter.4
  81.2 10.9 all-gather.6
  116.5 10.2 reduce-scatter.6
  138.0 10.9 all-gather.8
  159.7 10.2 reduce-scatter.8
  177.8 10.9 all-gather.10
  300.0 10.2 reduce-scatter.10
  317.1 131.2 all-reduce.3
where the time goes:
time: 470 us; the launch traced here: 462 us
  waiting for transfers between devices  176 us (37%)
  matrix products  151 us (32%)
  other arithmetic  44.7 us (10%)
  blocking collectives  41.6 us (9%)
  local copies, waits for them, and re-layouts  25.2 us (5%)
  between operations  14.7 us (3%)
  loops' own time  6.91 us (1%)
    psum x1, waiting for transfers between devices, per_device(): lax.psum((mixer_grads[0], mixer_grads[1], mixer_grads[2], mixer_grads[3],...  96 us
    psum x1, blocking collectives, per_device(): lax.psum((mixer_grads[0], mixer_grads[1], mixer_grads[2], mixer_grads[3],...  41.6 us
    dot_general x2, matrix products, one_block(): jnp.einsum('qhd,khd->hqk', grad_rows, values, preferred_element_type=jnp....  23.3 us
    dot_general x9, matrix products, times_transpose(): lax.dot_general(left, right, (((1,), (1,)), ((), ())), preferred_element_...  22.3 us
    dot_general x4, matrix products, score_block(): jnp.einsum('qhd,khd->hqk', query_rows, keys, preferred_element_type=jnp.f...  21.5 us
    convert_element_type x2, other arithmetic, one_block(): score_grad = (shares * (share_grad - jnp.sum(shares * share_grad, -1, kee...  19.2 us
    dot_general x1, matrix products, per_device(): jnp.dot(inner_low, outer_weight, preferred_element_type=jnp.float32)  17.3 us
    dot_general x2, matrix products, one_block(): jnp.einsum('hqk,qhd->khd', shares.astype(jnp.bfloat16), grad_rows, prefer...  15.8 us
  transfers between devices with their start and end apart: 9, of which 8 were waited for; matrix products, arithmetic and copies ran while one was open for 2% of the time, Pallas kernels for 0%

commit v1 on v0

--- a/solution.py
+++ b/solution.py
@@ -267,7 +267,7 @@
         tiled=True,
     ).astype(jnp.float32)
     input_grad = (first_grad + input_back).astype(jnp.bfloat16)
-    summed = lax.psum(
+    half = lax.psum(
         (
             mixer_grads[0],
             mixer_grads[1],
@@ -282,8 +282,9 @@
             second_gain_grad,
             second_shift_grad,
         ),
-        ("dp", "mp"),
-    )
+        "mp",
+    )
+    summed = lax.psum(half, "dp")
     ratios = jnp.sqrt(jnp.stack([mixer_square, dense_square]) / input_square)
     return (
         result.astype(jnp.bfloat16),

time: 470 us -> 452 us (0.962)
  waiting for transfers between devices: 176 us -> 78 us
  blocking collectives: 41.6 us -> 121 us
    psum x0 -> x2, blocking collectives: none -> 117 us  [the longest x1 76 us: per_device(): summed = lax.psum(half, 'dp')]
    psum x1, waiting for transfers between devices: 96 us -> 0.02 us  [per_device(): lax.psum((mixer_grads[0], mixer_grads[1], mixer_grads[2], mixer_grads[3],...]
    psum x1, blocking collectives: 41.6 us -> 3.44 us  [per_device(): lax.psum((mixer_grads[0], mixer_grads[1], mixer_grads[2], mixer_grads[3],...]
    all_gather x1, waiting for transfers between devices: 11.1 us -> 5.28 us  [per_device(): lax.all_gather(attended_grad, 'mp', axis=0, tiled=True)]
    unnamed x110 -> x102, local copies, waits for them, and re-layouts: 11.3 us -> 10.8 us
  transfers between devices with their start and end apart: 9 -> 10, of which waited for: 8 -> 8; matrix products, arithmetic and copies ran while one was open for 2% -> 25% of each run, Pallas kernels for 0% -> 0%
where the time goes in v1:
time: 452 us; the launch traced here: 443 us
  matrix products  151 us (33%)
  blocking collectives  121 us (27%)
  waiting for transfers between devices  78 us (17%)
  other arithmetic  44.9 us (10%)
  local copies, waits for them, and re-layouts  25 us (6%)
  between operations  15.2 us (3%)
  loops' own time  6.82 us (2%)
    psum x1, blocking collectives, per_device(): summed = lax.psum(half, 'dp')  76 us
    psum x1, blocking collectives, per_device(): lax.psum((mixer_square, dense_square, input_square), ('dp', 'mp'))  41.1 us
    dot_general x2, matrix products, one_block(): jnp.einsum('qhd,khd->hqk', grad_rows, values, preferred_element_type=jnp....  23.3 us
    dot_general x9, matrix products, times_transpose(): lax.dot_general(left, right, (((1,), (1,)), ((), ())), preferred_element_...  22.5 us
    dot_general x4, matrix products, score_block(): jnp.einsum('qhd,khd->hqk', query_rows, keys, preferred_element_type=jnp.f...  21.5 us
    convert_element_type x2, other arithmetic, one_block(): score_grad = (shares * (share_grad - jnp.sum(shares * share_grad, -1, kee...  19.3 us
    dot_general x1, matrix products, per_device(): jnp.dot(inner_low, outer_weight, preferred_element_type=jnp.float32)  17.3 us
    dot_general x2, matrix products, one_block(): jnp.einsum('hqk,qhd->khd', shares.astype(jnp.bfloat16), grad_rows, prefer...  15.7 us
  transfers between devices with their start and end apart: 10, of which 8 were waited for; matrix products, arithmetic and copies ran while one was open for 25% of the time, Pallas kernels for 0%

profile of v1, /device:TPU:0, one launch (start us, length us, event | category | flops | bytes accessed | tf_op | source)
XLA Modules:
  0.0 442.7 jit_solution(10218108139405424064)
XLA Ops:
  8.0 14.1 %all-gather.5.cloned.1.call-done = bf16[1024,768]{1,0:T(8,128)(2,1)} async-done(((bf16[512,768]{1,0:T(8,128)(2,1)}), bf16[1024,768]{1,0:T(8,128)(2,1)}) %all-gather.5.cloned.1.call-update) | async-done | bytes 1572880 | tf_op jit(solution)/shard_map/all_gather | solution.py:176
  22.1 3.4 convolution_convert_fusion.4
  29.1 27.5 %while.27 = (s32[]{:T(128)}, bf16[2,512,6,64]{1,3,2,0:T(8,128)(2,1)}, f32[2,6,512]{2,1,0:T(8,128)S(1)}, s32[2]{0:T(128)S(1)}, s32[1024]{0:T(1024)S(1)}, /*index=...) while((s32[]{:T(128)}, ...), condition=%wide.region_3.4_spmd, body=%wide.region_0.3_spmd.sunk | while | flops 843772928 | bytes 45472476 | solution.py:97
  30.8 3.4 fusion.212
  34.2 3.6 fusion.213
  37.8 5.0 %fusion.214 = bf16[2,512,6,64]{1,3,2,0:T(8,128)(2,1)} fusion(bf16[2,512,6,64]{1,3,2,0:T(8,128)(2,1)} %get-tuple-element.420, s32[]{:T(128)} %get-tuple-element.419, bf16[1024,6,64]{0,2,1:T(8,128)(2,1)S(1)} %copy-done.9, f32[6,512,1024]{2,1,0:T(8,128)S(1)} %get-tuple-element.390, f32[6,512]{1,0:T(8,128)S(1)} %fusion.213, ...), kind=kOutput, calls=%fused_computation.8.clone.1 | convolution fusion | flops 418578432 | bytes 14311936 | tf_op jit(solution)/shard_map/while/body/eval_jaxpr/hqk,khd->qhd/dot_general | solution.py:94
  44.5 3.4 fusion.212
  47.9 3.6 fusion.213
  51.6 5.0 %fusion.214 = bf16[2,512,6,64]{1,3,2,0:T(8,128)(2,1)} fusion(bf16[2,512,6,64]{1,3,2,0:T(8,128)(2,1)} %get-tuple-element.420, s32[]{:T(128)} %get-tuple-element.419, bf16[1024,6,64]{0,2,1:T(8,128)(2,1)S(1)} %copy-done.9, f32[6,512,1024]{2,1,0:T(8,128)S(1)} %get-tuple-element.390, f32[6,512]{1,0:T(8,128)S(1)} %fusion.213, ...), kind=kOutput, calls=%fused_computation.8.clone.1 | convolution fusion | flops 418578432 | bytes 14311936 | tf_op jit(solution)/shard_map/while/body/eval_jaxpr/hqk,khd->qhd/dot_general | solution.py:94
  56.6 2.0 copy.36
  58.8 2.7 fusion.146
  61.6 12.1 %reduce-scatter.5.cloned.1.call-done = f32[512,768]{1,0:T(8,128)} async-done(((f32[1024,768]{1,0:T(8,128)}), f32[512,768]{1,0:T(8,128)}) %reduce-scatter.5.cloned.1.call-update) | async-done | bytes 1572880 | tf_op jit(solution)/shard_map/reduce_scatter | solution.py:190
  73.7 1.8 convolution_add_fusion.3
  75.5 3.1 fusion.144
  81.2 10.9 %all-gather.7.cloned.1.call-done = bf16[1024,768]{1,0:T(8,128)(2,1)} async-done(((bf16[512,768]{1,0:T(8,128)(2,1)}), bf16[1024,768]{1,0:T(8,128)(2,1)}) %all-gather.7.cloned.1.call-update) | async-done | bytes 1572880 | tf_op jit(solution)/shard_map/all_gather | solution.py:205
  92.1 4.2 fusion.147
  96.2 2.7 copy-done.52
  98.9 17.3 %fusion.53 = bf16[1024,768]{1,0:T(8,128)(2,1)} fusion(bf16[1536,768]{1,0:T(8,128)(2,1)S(1)} %copy-done.48, f32[1024,1536]{1,0:T(8,128)S(1)} %fusion.147), kind=kOutput, calls=%fused_computation.78 | convolution fusion | flops 2518941696 | bytes 10223616 | tf_op jit(solution)/shard_map/dot_general | solution.py:211
  116.4 10.3 %reduce-scatter.7.cloned.1.call-done = bf16[512,768]{1,0:T(8,128)(2,1)} async-done(((bf16[1024,768]{1,0:T(8,128)(2,1)}), bf16[512,768]{1,0:T(8,128)(2,1)}) %reduce-scatter.7.cloned.1.call-update) | async-done | bytes 786448 | tf_op jit(solution)/shard_map/reduce_scatter | solution.py:210
  128.2 3.5 fusion.143
  137.4 11.1 %all-gather.9.cloned.1.call-done = bf16[1024,768]{1,0:T(8,128)(2,1)} async-done(((bf16[512,768]{1,0:T(8,128)(2,1)}), bf16[1024,768]{1,0:T(8,128)(2,1)}) %all-gather.9.cloned.1.call-update) | async-done | bytes 1572880 | tf_op jit(solution)/shard_map/all_gather | solution.py:235
  148.5 10.5 %convolution_convert_fusion = bf16[1024,768]{1,0:T(8,128)(2,1)} fusion(bf16[768,1536]{1,0:T(8,128)(2,1)S(1)} %copy-done, f32[1024,1536]{1,0:T(8,128)} %copy-done.52, bf16[1024,768]{1,0:T(8,128)(2,1)} %all-gather.9.cloned.1.call-done, bf16[1536,768]{1,0:T(8,128)(2,1)} %param.32), kind=kOutput, calls=%fused_computation.79 | convolution fusion | flops 4848353280 | bytes 14155776 | tf_op jit(solution)/shard_map/dot_general | solution.py:23
  159.3 10.1 %reduce-scatter.9.cloned.1.call-done = bf16[512,768]{1,0:T(8,128)(2,1)} async-done(((bf16[1024,768]{1,0:T(8,128)(2,1)}), bf16[512,768]{1,0:T(8,128)(2,1)}) %reduce-scatter.9.cloned.1.call-update) | async-done | bytes 786448 | tf_op jit(solution)/shard_map/reduce_scatter | solution.py:238
  169.4 4.1 multiply_reduce_fusion.3
  178.2 2.6 fusion.102
  183.1 5.3 %all-gather.11.cloned.1.call-done = bf16[1024,768]{1,0:T(8,128)(2,1)} async-done(((bf16[512,768]{1,0:T(8,128)(2,1)}), bf16[1024,768]{1,0:T(8,128)(2,1)}) %all-gather.11.cloned.1.call-update) | async-done | bytes 1572880 | tf_op jit(solution)/shard_map/all_gather | solution.py:251
  188.4 3.1 convolution_convert_fusion.1
  192.4 99.0 %while.28 = (s32[]{:T(128)}, f32[1024,6,64]{0,2,1:T(8,128)S(1)}, f32[1024,6,64]{0,2,1:T(8,128)}, bf16[2,512,6,64]{1,3,2,0:T(8,128)(2,1)}, s32[2]{0:T(128)S(1)}, ...) while((s32[]{:T(128)}, f32[1024,6,64]{0,2,1:T(8,128)S(1)}, ...), condition=%wide.region_17.18_spmd.clone, body=%wide.region_15.17_spmd.clone.sunk | while | flops 2063332352 | bytes 179538384 | solution.py:135
  193.7 7.4 %fusion.224 = f32[6,512,1024]{2,1,0:T(8,128)} fusion(bf16[1024,6,64]{0,2,1:T(8,128)(2,1)S(1)} %get-tuple-element.487, bf16[1024,6,64]{0,2,1:T(8,128)(2,1)} %get-tuple-element.484, s32[]{:T(128)S(6)} %select_n.64), kind=kOutput, calls=%fused_computation.33.clone.1 | convolution fusion | flops 402653184 | bytes 13762564 | tf_op jit(solution)/shard_map/while/body/eval_jaxpr/qhd,khd->hqk/dot_general | solution.py:76
  203.5 11.7 %multiply_reduce_fusion.9 = (f32[6,512]{1,0:T(8,128)S(1)}, f32[6,512,1024]{2,1,0:T(8,128)}) fusion(f32[6,512,1024]{2,1,0:T(8,128)} %fusion.224, f32[6,512]{1,0:T(8,128)S(1)} %dynamic-slice_bitcast_fusion.2, pred[512,1024]{1,0:T(8,128)(4,1)S(1)} %broadcast_compare_fusion.5, bf16[1024,6,64]{0,2,1:T(8,128)(2,1)} %get-tuple-element.490, ...), kind=kOutput, calls=%fused_computation.17.clone.1 | convolution fusion | flops 418378752 | bytes 26894340 | tf_op jit(solution)/shard_map/while/body/eval_jaxpr/qhd,khd->hqk/dot_general | solution.py:118
  216.7 9.6 %multiply_convert_fusion.2 = bf16[6,512,1024]{2,1,0:T(8,128)(2,1)} fusion(f32[6,512,1024]{2,1,0:T(8,128)} %get-tuple-element.404, f32[6,512,1024]{2,1,0:T(8,128)S(1)} %bitcast.121, f32[6,512]{1,0:T(8,128)S(1)} %get-tuple-element.405, f32[6,512]{1,0:T(8,128)S(1)} %dynamic-slice_bitcast_fusion.2, pred[512,1024]{1,0:T(8,128)(4,1)S(1)} %broadcast_compare_fusion.5), kind=kLoop, calls=%fused_computation.16.clone.1 | loop fusion | flops 18874368 | bytes 32006144 | tf_op jit(solution)/shard_map/while/body/eval_jaxpr/convert_element_type | solution.py:123
  226.3 4.4 bitcast_add_fusion.4
  231.2 2.0 fusion.225
  234.1 7.6 %bitcast_add_fusion.5 = f32[1024,6,64]{0,2,1:T(8,128)} fusion(f32[1024,6,64]{0,2,1:T(8,128)} %get-tuple-element.464, f32[6,512,1024]{2,1,0:T(8,128)} %fusion.224, f32[6,512]{1,0:T(8,128)S(1)} %dynamic-slice_bitcast_fusion.2, pred[512,1024]{1,0:T(8,128)(4,1)S(1)} %broadcast_compare_fusion.5, pred[]{:T(512)S(6)} %compare.3, ...), kind=kOutput, calls=%fused_computation.22.clone.1 | convolution fusion | flops 416022528 | bytes 16662533 | tf_op jit(solution)/shard_map/while/body/eval_jaxpr/hqk,qhd->khd/dot_general | solution.py:112
  243.0 7.4 %fusion.224 = f32[6,512,1024]{2,1,0:T(8,128)} fusion(bf16[1024,6,64]{0,2,1:T(8,128)(2,1)S(1)} %get-tuple-element.487, bf16[1024,6,64]{0,2,1:T(8,128)(2,1)} %get-tuple-element.484, s32[]{:T(128)S(6)} %select_n.64), kind=kOutput, calls=%fused_computation.33.clone.1 | convolution fusion | flops 402653184 | bytes 13762564 | tf_op jit(solution)/shard_map/while/body/eval_jaxpr/qhd,khd->hqk/dot_general | solution.py:76
  252.8 11.6 %multiply_reduce_fusion.9 = (f32[6,512]{1,0:T(8,128)S(1)}, f32[6,512,1024]{2,1,0:T(8,128)}) fusion(f32[6,512,1024]{2,1,0:T(8,128)} %fusion.224, f32[6,512]{1,0:T(8,128)S(1)} %dynamic-slice_bitcast_fusion.2, pred[512,1024]{1,0:T(8,128)(4,1)S(1)} %broadcast_compare_fusion.5, bf16[1024,6,64]{0,2,1:T(8,128)(2,1)} %get-tuple-element.490, ...), kind=kOutput, calls=%fused_computation.17.clone.1 | convolution fusion | flops 418378752 | bytes 26894340 | tf_op jit(solution)/shard_map/while/body/eval_jaxpr/qhd,khd->hqk/dot_general | solution.py:118
  265.7 9.6 %multiply_convert_fusion.2 = bf16[6,512,1024]{2,1,0:T(8,128)(2,1)} fusion(f32[6,512,1024]{2,1,0:T(8,128)} %get-tuple-element.404, f32[6,512,1024]{2,1,0:T(8,128)S(1)} %bitcast.121, f32[6,512]{1,0:T(8,128)S(1)} %get-tuple-element.405, f32[6,512]{1,0:T(8,128)S(1)} %dynamic-slice_bitcast_fusion.2, pred[512,1024]{1,0:T(8,128)(4,1)S(1)} %broadcast_compare_fusion.5), kind=kLoop, calls=%fused_computation.16.clone.1 | loop fusion | flops 18874368 | bytes 32006144 | tf_op jit(solution)/shard_map/while/body/eval_jaxpr/convert_element_type | solution.py:123
  275.4 4.4 bitcast_add_fusion.4
  280.2 2.0 fusion.225
  283.2 8.1 %bitcast_add_fusion.5 = f32[1024,6,64]{0,2,1:T(8,128)} fusion(f32[1024,6,64]{0,2,1:T(8,128)} %get-tuple-element.464, f32[6,512,1024]{2,1,0:T(8,128)} %fusion.224, f32[6,512]{1,0:T(8,128)S(1)} %dynamic-slice_bitcast_fusion.2, pred[512,1024]{1,0:T(8,128)(4,1)S(1)} %broadcast_compare_fusion.5, pred[]{:T(512)S(6)} %compare.3, ...), kind=kOutput, calls=%fused_computation.22.clone.1 | convolution fusion | flops 416022528 | bytes 16662533 | tf_op jit(solution)/shard_map/while/body/eval_jaxpr/hqk,qhd->khd/dot_general | solution.py:112
  291.5 2.0 copy.37
  297.5 2.3 add_convert_fusion
  300.4 41.1 %all-reduce = (f32[1]{0:T(128)}, f32[1]{0:T(128)}, f32[]{:T(128)}) all-reduce(f32[1]{0:T(128)} %bitcast.13, f32[1]{0:T(128)} %bitcast.12, f32[]{:T(128)} %get-tuple-element.263), channel_id=1, replica_groups=mesh['dp'=16,'mp'=2] {'dp','mp'}, use_global_device_ids=true, to_apply=%region_54.55 | all-reduce | flops 3 | bytes 24 | tf_op jit(solution)/shard_map/psum | solution.py:225
  341.6 2.5 fusion.96
  344.2 3.4 all-reduce.3
  347.6 76.0 %all-reduce.1 = (f32[64]{0:T(128)}, f32[768]{0:T(1024)}, f32[64]{0:T(128)}, f32[768]{0:T(1024)}, f32[768]{0:T(1024)}, /*index=5*/f32[768]{0:T(1024)}, f32[768]{0:T(1024)}, f32[768]{0:T(1024)}) all-reduce(f32[64]{0:T(128)S(1)} %get-tuple-element.237, f32[768]{0:T(1024)S(1)} %get-tuple-element.238, ...), channel_id=1, replica_groups=mesh['dp'=16,'mp'=2] {'dp'}, use_global_device_ids=true, to_apply=%region_23.24 | all-reduce | flops 4736 | bytes 37888 | tf_op jit(solution)/shard_map/psum | solution.py:287
  423.6 2.6 add_convert_fusion.1
  426.2 2.8 all-reduce.8.cloned.1.call-done
  (215 shorter events, 43.2 us)
Async XLA Ops:
  7.2 84.9 %copy-start = (bf16[768,1536]{1,0:T(8,128)(2,1)S(1)}, bf16[768,1536]{1,0:T(8,128)(2,1)}, u32[]{:S(2)}) copy-start(bf16[768,1536]{1,0:T(8,128)(2,1)} %param.31) | copy-start | bytes 7077892
  7.2 14.9 %all-gather.5.cloned.1.call-start = ((), (), s32[]{:S(2)}) async-start(), calls=%async_computation.4 | async-start | bytes 2359296 | tf_op jit(solution)/shard_map/all_gather | solution.py:176
  7.9 65.8 %reduce-scatter.5.cloned.1.call-start = ((), (), s32[]{:S(2)}) async-start(), calls=%async_computation.5 | async-start | bytes 4718592 | tf_op jit(solution)/shard_map/reduce_scatter | solution.py:190
  22.1 4.3 copy-start.23
  34.2 3.7 copy-start.9
  47.9 3.7 copy-start.9
  58.8 15.0 %copy-start.27 = (bf16[768,64]{0,1:T(8,128)(2,1)S(1)}, bf16[768,64]{0,1:T(8,128)(2,1)}, u32[]{:S(2)}) copy-start(bf16[768,64]{0,1:T(8,128)(2,1)} %param.33) | copy-start | bytes 294916
  61.5 14.0 %copy-start.32 = (bf16[64,768]{1,0:T(8,128)(2,1)S(1)}, bf16[64,768]{1,0:T(8,128)(2,1)}, u32[]{:S(2)}) copy-start(bf16[64,768]{1,0:T(8,128)(2,1)} %param.35) | copy-start | bytes 294916
  61.5 30.6 %all-gather.7.cloned.1.call-start = ((), (), s32[]{:S(2)}) async-start(), calls=%async_computation.6 | async-start | bytes 2359296 | tf_op jit(solution)/shard_map/all_gather | solution.py:205
  81.0 45.7 %reduce-scatter.7.cloned.1.call-start = ((), (), s32[]{:S(2)}) async-start(), calls=%async_computation.7 | async-start | bytes 2359296 | tf_op jit(solution)/shard_map/reduce_scatter | solution.py:210
  92.1 6.8 %copy-start.48 = (bf16[1536,768]{1,0:T(8,128)(2,1)S(1)}, bf16[1536,768]{1,0:T(8,128)(2,1)}, u32[]{:S(2)}) copy-start(bf16[1536,768]{1,0:T(8,128)(2,1)} %param.32) | copy-start | bytes 7077892
  98.9 17.4 %copy-start.51 = (bf16[64]{0:T(256)(128)(2,1)S(1)}, bf16[64]{0:T(256)(128)(2,1)}, u32[]{:S(2)}) copy-start(bf16[64]{0:T(256)(128)(2,1)} %param.38) | copy-start | bytes 388
  98.9 17.5 %copy-start.43 = (bf16[768]{0:T(1024)(128)(2,1)S(1)}, bf16[768]{0:T(1024)(128)(2,1)}, u32[]{:S(2)}) copy-start(bf16[768]{0:T(1024)(128)(2,1)} %param.40) | copy-start | bytes 4612
  98.9 17.5 %copy-start.44 = (bf16[768]{0:T(1024)(128)(2,1)S(1)}, bf16[768]{0:T(1024)(128)(2,1)}, u32[]{:S(2)}) copy-start(bf16[768]{0:T(1024)(128)(2,1)} %param.43) | copy-start | bytes 4612
  98.9 17.5 %copy-start.45 = (bf16[768]{0:T(1024)(128)(2,1)S(1)}, bf16[768]{0:T(1024)(128)(2,1)}, u32[]{:S(2)}) copy-start(bf16[768]{0:T(1024)(128)(2,1)} %param.44) | copy-start | bytes 4612
  98.9 27.8 %copy-start.25 = (bf16[768,64]{0,1:T(8,128)(2,1)S(1)}, bf16[768,64]{0,1:T(8,128)(2,1)}, u32[]{:S(2)}) copy-start(bf16[768,64]{0,1:T(8,128)(2,1)} %param.37) | copy-start | bytes 294916
  116.3 32.2 %all-gather.9.cloned.1.call-start = ((), (), s32[]{:S(2)}) async-start(), calls=%async_computation.8 | async-start | bytes 2359296 | tf_op jit(solution)/shard_map/all_gather | solution.py:235
  128.2 3.8 copy-start.12
  137.4 32.0 %reduce-scatter.9.cloned.1.call-start = ((), (), s32[]{:S(2)}) async-start(), calls=%async_computation.9 | async-start | bytes 2359296 | tf_op jit(solution)/shard_map/reduce_scatter | solution.py:238
  159.0 14.5 %copy-start.4 = (f32[512,768]{1,0:T(8,128)S(1)}, f32[512,768]{1,0:T(8,128)}, u32[]{:S(2)}) copy-start(f32[512,768]{1,0:T(8,128)} %copy-done.3) | copy-start | bytes 4718596
  159.0 29.3 %all-gather.11.cloned.1.call-start = ((), (), s32[]{:S(2)}) async-start(), calls=%async_computation.10 | async-start | bytes 2359296 | tf_op jit(solution)/shard_map/all_gather | solution.py:251
  169.4 4.1 copy-start.8
  169.4 4.1 copy-start.16
  177.2 122.7 %all-reduce.10.cloned.1.call-start = ((), (), s32[]{:S(2)}) async-start(), calls=%async_computation.13 | async-start | bytes 1572864 | tf_op jit(solution)/shard_map/psum | solution.py:270
  177.3 4.5 %copy-start.6 = (f32[512,768]{1,0:T(8,128)S(1)}, f32[512,768]{1,0:T(8,128)}, u32[]{:S(2)}) copy-start(f32[512,768]{1,0:T(8,128)} %copy-done.5) | copy-start | bytes 4718596
  180.9 7.5 %copy-start.19 = (bf16[384,768]{1,0:T(8,128)(2,1)S(1)}, bf16[384,768]{1,0:T(8,128)(2,1)}, u32[]{:S(2)}) copy-start(bf16[384,768]{1,0:T(8,128)(2,1)} %param.30) | copy-start | bytes 1769476
  183.0 9.4 %copy-start.30 = (f32[2,6,512]{2,1,0:T(8,128)S(1)}, f32[2,6,512]{2,1,0:T(8,128)}, u32[]{:S(2)}) copy-start(f32[2,6,512]{2,1,0:T(8,128)} %copy-done.29) | copy-start | bytes 73732
  183.0 240.6 %reduce-scatter.11.cloned.1.call-start = ((), (), s32[]{:S(2)}) async-start(), calls=%async_computation.11 | async-start | bytes 2359296 | tf_op jit(solution)/shard_map/reduce_scatter | solution.py:263
  203.4 11.7 %slice-start = ((s8[12582912]{0:T(1024)(128)(4,1)}), s8[4194304]{0:T(1024)(128)(4,1)S(1)}, s32[]{:S(2)}) async-start(s8[12582912]{0:T(1024)(128)(4,1)} %bitcast.120), calls=%async_computation.14 | async-start | bytes 8388608 | tf_op jit(solution)/shard_map/while
  203.4 11.7 %slice-start.1 = ((s8[12582912]{0:T(1024)(128)(4,1)}), s8[4194304]{0:T(1024)(128)(4,1)S(1)}, s32[]{:S(2)}) async-start(s8[12582912]{0:T(1024)(128)(4,1)} %bitcast.120), calls=%async_computation.15 | async-start | bytes 8388608 | tf_op jit(solution)/shard_map/while
  203.5 13.2 %slice-start.2 = ((s8[12582912]{0:T(1024)(128)(4,1)}), s8[4194304]{0:T(1024)(128)(4,1)S(1)}, s32[]{:S(2)}) async-start(s8[12582912]{0:T(1024)(128)(4,1)} %bitcast.120), calls=%async_computation.16 | async-start | bytes 8388608 | tf_op jit(solution)/shard_map/while
  226.3 4.7 %copy-start.2 = (bf16[6,512,1024]{2,1,0:T(8,128)(2,1)S(1)}, bf16[6,512,1024]{2,1,0:T(8,128)(2,1)}, u32[]{:S(2)}) copy-start(bf16[6,512,1024]{2,1,0:T(8,128)(2,1)} %multiply_convert_fusion.2) | copy-start | bytes 18874372 | tf_op jit(solution)/shard_map/while
  226.3 4.9 %copy-start.14 = (bf16[2,512,6,64]{1,3,2,0:T(8,128)(2,1)S(1)}, bf16[2,512,6,64]{1,3,2,0:T(8,128)(2,1)}, u32[]{:S(2)}) copy-start(bf16[2,512,6,64]{1,3,2,0:T(8,128)(2,1)} %get-tuple-element.465) | copy-start | bytes 2359300 | tf_op jit(solution)/shard_map/while
  252.7 11.7 %slice-start = ((s8[12582912]{0:T(1024)(128)(4,1)}), s8[4194304]{0:T(1024)(128)(4,1)S(1)}, s32[]{:S(2)}) async-start(s8[12582912]{0:T(1024)(128)(4,1)} %bitcast.120), calls=%async_computation.14 | async-start | bytes 8388608 | tf_op jit(solution)/shard_map/while
  252.7 11.7 %slice-start.1 = ((s8[12582912]{0:T(1024)(128)(4,1)}), s8[4194304]{0:T(1024)(128)(4,1)S(1)}, s32[]{:S(2)}) async-start(s8[12582912]{0:T(1024)(128)(4,1)} %bitcast.120), calls=%async_computation.15 | async-start | bytes 8388608 | tf_op jit(solution)/shard_map/while
  252.7 13.0 %slice-start.2 = ((s8[12582912]{0:T(1024)(128)(4,1)}), s8[4194304]{0:T(1024)(128)(4,1)S(1)}, s32[]{:S(2)}) async-start(s8[12582912]{0:T(1024)(128)(4,1)} %bitcast.120), calls=%async_computation.16 | async-start | bytes 8388608 | tf_op jit(solution)/shard_map/while
  275.4 4.7 %copy-start.2 = (bf16[6,512,1024]{2,1,0:T(8,128)(2,1)S(1)}, bf16[6,512,1024]{2,1,0:T(8,128)(2,1)}, u32[]{:S(2)}) copy-start(bf16[6,512,1024]{2,1,0:T(8,128)(2,1)} %multiply_convert_fusion.2) | copy-start | bytes 18874372 | tf_op jit(solution)/shard_map/while
  275.4 4.9 %copy-start.14 = (bf16[2,512,6,64]{1,3,2,0:T(8,128)(2,1)S(1)}, bf16[2,512,6,64]{1,3,2,0:T(8,128)(2,1)}, u32[]{:S(2)}) copy-start(bf16[2,512,6,64]{1,3,2,0:T(8,128)(2,1)} %get-tuple-element.465) | copy-start | bytes 2359300 | tf_op jit(solution)/shard_map/while
  297.4 46.7 %copy-start.34 = (f32[768]{0:T(1024)S(1)}, f32[768]{0:T(1024)}, u32[]{:S(2)}) copy-start(f32[768]{0:T(1024)} %get-tuple-element.174) | copy-start | bytes 9220
  297.4 46.7 %copy-start.35 = (f32[768]{0:T(1024)S(1)}, f32[768]{0:T(1024)}, u32[]{:S(2)}) copy-start(f32[768]{0:T(1024)} %get-tuple-element.179) | copy-start | bytes 9220
  297.4 46.7 %copy-start.36 = (f32[768]{0:T(1024)S(1)}, f32[768]{0:T(1024)}, u32[]{:S(2)}) copy-start(f32[768]{0:T(1024)} %get-tuple-element.171) | copy-start | bytes 9220
  297.4 46.7 %copy-start.37 = (f32[768]{0:T(1024)S(1)}, f32[768]{0:T(1024)}, u32[]{:S(2)}) copy-start(f32[768]{0:T(1024)} %get-tuple-element.176) | copy-start | bytes 9220
  297.5 46.7 %copy-start.38 = (f32[768]{0:T(1024)S(1)}, f32[768]{0:T(1024)}, u32[]{:S(2)}) copy-start(f32[768]{0:T(1024)} %get-tuple-element.177) | copy-start | bytes 9220
  297.5 46.7 %copy-start.39 = (f32[768]{0:T(1024)S(1)}, f32[768]{0:T(1024)}, u32[]{:S(2)}) copy-start(f32[768]{0:T(1024)} %get-tuple-element.249) | copy-start | bytes 9220
  297.5 46.7 %copy-start.46 = (f32[64]{0:T(128)S(1)}, f32[64]{0:T(128)}, u32[]{:S(2)}) copy-start(f32[64]{0:T(128)} %get-tuple-element.266) | copy-start | bytes 772
  297.5 46.7 %copy-start.47 = (f32[64]{0:T(128)S(1)}, f32[64]{0:T(128)}, u32[]{:S(2)}) copy-start(f32[64]{0:T(128)} %get-tuple-element.264) | copy-start | bytes 772
  299.8 135.6 %copy-start.1 = (bf16[768,1536]{1,0:T(8,128)(2,1)S(1)}, bf16[768,1536]{1,0:T(8,128)(2,1)}, u32[]{:S(2)}) copy-start(bf16[768,1536]{1,0:T(8,128)(2,1)} %param.31) | copy-start | bytes 7077892
  299.9 129.1 %all-reduce.8.cloned.1.call-start = ((), (), s32[]{:S(2)}) async-start(), calls=%async_computation.12 | async-start | bytes 1572864 | tf_op jit(solution)/shard_map/psum | solution.py:287
  (26 other events, 60.8 us)
Sparse Core Ops, SparseCore 0:
  9.6 12.4 all-gather.4
  61.6 12.0 reduce-scatter.4
  81.1 10.9 all-gather.6
  116.4 10.2 reduce-scatter.6
  137.5 10.9 all-gather.8
  159.1 10.2 reduce-scatter.8
  177.3 10.9 all-gather.10
  192.2 20.4 all-reduce.9
  300.0 10.2 reduce-scatter.10
  316.5 112.4 all-reduce.7
